TPU v7x, 256 devices: a whole 4x4x8 slice. The times are simulated.
256 devices in a mesh: shard: 16 (over y, z_hi, core), rep: 16 (over x, z_lo).
Axes of the slice: x: 4, y: 4, z: 8 (z_hi: 2, z_lo: 4; z = z_hi * 4 + z_lo), core: 2. Of those that a mesh axis runs over, the one named last changes fastest.
Arguments:
- inputs: bfloat16 [50432, 768], P(('shard', 'rep')), may hold values from -6 to 6
- norm1_gain: float32 [768], replicated, may hold values from 0.25 to 1.75
- w_qkv: bfloat16 [768, 2304], P('shard'), may hold values from -0.21875 to 0.21875
- w_proj: bfloat16 [768, 768], P('shard'), may hold values from -0.875 to 0.875
- norm2_gain: float32 [768], replicated, may hold values from 0.25 to 1.75
- w_router: bfloat16 [768, 32], P('shard'), may hold values from -0.21875 to 0.21875
- w_expert_in: bfloat16 [2, 768, 3072], P(None, 'shard'), may hold values from -0.21875 to 0.21875
- w_expert_out: bfloat16 [2, 3072, 768], P(None, 'shard'), may hold values from -0.875 to 0.875
- expert_ids: int32 [50432, 2], P(('shard', 'rep')), may hold values from 0 to 1, all different within a row
- capacity: int32 [2], replicated, may hold values from 64 to 128, as said below
- cotangent: bfloat16 [50432, 768], P(('shard', 'rep')), may hold values from -6 to 6
Outputs:
- outputs: bfloat16 [50432, 768], P(('shard', 'rep'))
- grad_inputs: float32 [50432, 768], P(('shard', 'rep'))
- grad_norm1_gain: float32 [768], replicated
- grad_qkv: float32 [768, 2304], P('shard')
- grad_proj: float32 [768, 768], P('shard')
- grad_norm2_gain: float32 [768], replicated
- grad_router: float32 [768, 32], P('shard')
- grad_expert_in: float32 [2, 768, 3072], P(None, 'shard')
- grad_expert_out: float32 [2, 3072, 768], P(None, 'shard')
Inputs may be any that keep to these rules, and one draw needn't show every extreme that they name: Every expert's capacity is 64 to 128; some expert has exactly 128. `expert_ids`: the two experts of a token differ.
All inputs are finite; a program needn't handle non-finite values.
Results may differ from a plain program's by a relative error of at most 0.025.
Values may be sent and summed in bfloat16 or wider, within the bound.
No kernel may reach another device: no remote copies, remote signals or barrier semaphores. Data moves between devices by JAX's collectives and lax.ppermute only.
A program may use at most 128 MiB of HBM per device.

v0:
```python
import jax
import jax.numpy as jnp
from jax import lax
from jax.sharding import PartitionSpec as P

HEADS = 12
HD = 64
EXPERTS = 32
E_WIN = 2
SEQ = 197
CAP = 128
EPS = 1e-06


def layer_norm(values, gain):
    centred = values - jnp.mean(values, axis=-1, keepdims=True)
    inverse = lax.rsqrt(jnp.mean(centred * centred, axis=-1, keepdims=True) + EPS)
    normed = centred * inverse
    return (normed, inverse, (normed * gain).astype(jnp.bfloat16))


def layer_norm_back(grad_out, normed, inverse, gain):
    scaled = grad_out * gain
    grad_in = inverse * (
        scaled
        - jnp.mean(scaled, axis=-1, keepdims=True)
        - normed * jnp.mean(scaled * normed, axis=-1, keepdims=True)
    )
    return (grad_in, jnp.sum(grad_out * normed, axis=0))


def butterfly_sum(value, axis, size, wire=None):
    step = 1
    while step < size:
        pairs = [(i, i ^ step) for i in range(size)]
        sent = value if wire is None else value.astype(wire)
        other = lax.ppermute(sent, axis, pairs)
        value = sent.astype(jnp.float32) + other.astype(jnp.float32)
        step *= 2
    return value


def heads_view(block, images):
    return block.reshape(images, SEQ, HEADS, HD)


def attention_scores(qkv, images):
    width = HEADS * HD
    query = heads_view(qkv[:, :width], images)
    keys = heads_view(qkv[:, width : 2 * width], images)
    values = heads_view(qkv[:, 2 * width :], images)
    scores = jnp.einsum(
        "bqhd,bkhd->bhqk", query, keys, preferred_element_type=jnp.float32
    ) * HD ** (-0.5)
    return (query, keys, values, scores)


def attention_forward(qkv, images):
    query, keys, values, scores = attention_scores(qkv, images)
    logsum = jax.nn.logsumexp(scores, axis=-1, keepdims=True)
    probs = jnp.exp(scores - logsum).astype(jnp.bfloat16)
    mixed = jnp.einsum("bhqk,bkhd->bqhd", probs, values, preferred_element_type=jnp.float32).astype(
        jnp.bfloat16
    )
    return (mixed.reshape(images * SEQ, HEADS * HD), logsum)


def attention_backward(qkv, mixed, logsum, grad_mixed, images):
    query, keys, values, scores = attention_scores(qkv, images)
    probs_full = jnp.exp(scores - logsum)
    probs = probs_full.astype(jnp.bfloat16)
    grad_out = heads_view(grad_mixed, images)
    out_rows = heads_view(mixed, images)
    grad_values = jnp.einsum("bhqk,bqhd->bkhd", probs, grad_out, preferred_element_type=jnp.float32)
    grad_probs = jnp.einsum("bqhd,bkhd->bhqk", grad_out, values, preferred_element_type=jnp.float32)
    delta = jnp.sum(grad_out.astype(jnp.float32) * out_rows.astype(jnp.float32), axis=-1)
    delta = jnp.transpose(delta, (0, 2, 1))[..., None]
    grad_scores = (probs_full * (grad_probs - delta)).astype(jnp.bfloat16)
    scale = HD ** (-0.5)
    grad_query = (
        jnp.einsum("bhqk,bkhd->bqhd", grad_scores, keys, preferred_element_type=jnp.float32) * scale
    )
    grad_keys = (
        jnp.einsum("bhqk,bqhd->bkhd", grad_scores, query, preferred_element_type=jnp.float32)
        * scale
    )
    width = HEADS * HD
    rows = images * SEQ
    return jnp.concatenate(
        [
            grad_query.reshape(rows, width),
            grad_keys.reshape(rows, width),
            grad_values.reshape(rows, width),
        ],
        axis=1,
    ).astype(jnp.bfloat16)


def route_masks(expert_ids, capacity):
    count = expert_ids.shape[0]
    picked_hot = (expert_ids[:, :, None] == jnp.arange(E_WIN)[None, None, :]).astype(jnp.int32)
    ordered = jnp.transpose(picked_hot, (1, 0, 2)).reshape(2 * count, E_WIN)
    before = jnp.cumsum(ordered, axis=0) - ordered
    position = jnp.sum(before * ordered, axis=1).reshape(2, count).T
    limit = jnp.sum(picked_hot * capacity[None, None, :], axis=2)
    kept_mask = (position < limit).astype(jnp.float32)
    slot_hot = (position[:, :, None] == jnp.arange(CAP)[None, None, :]).astype(jnp.float32)
    return (
        kept_mask[:, :, None, None]
        * picked_hot.astype(jnp.float32)[:, :, :, None]
        * slot_hot[:, :, None, :]
    )


def body(
    inputs,
    norm1_gain,
    w_qkv,
    w_proj,
    norm2_gain,
    w_router,
    w_expert_in,
    w_expert_out,
    expert_ids,
    capacity,
    cotangent,
):
    high = lax.Precision.HIGHEST
    images = inputs.shape[0] // SEQ
    shard_rows = w_qkv.shape[0]
    hid_rows = w_expert_out.shape[1]
    width = HEADS * HD
    dense_all = lax.all_gather(
        jnp.concatenate([w_qkv, w_proj, w_router], axis=1), "shard", axis=0, tiled=True
    )
    full_qkv, full_proj, full_router = (
        dense_all[:, : 3 * width],
        dense_all[:, 3 * width : 4 * width],
        dense_all[:, 4 * width :],
    )
    x_float = inputs.astype(jnp.float32)
    normed1, inverse1, hidden1 = layer_norm(x_float, norm1_gain)
    qkv = jnp.dot(hidden1, full_qkv, preferred_element_type=jnp.float32).astype(jnp.bfloat16)
    mixed, logsum = attention_forward(qkv, images)
    attended = x_float + jnp.dot(mixed, full_proj, preferred_element_type=jnp.float32)
    normed2, inverse2, hidden2 = layer_norm(attended, norm2_gain)
    logits = jnp.dot(hidden2, full_router, preferred_element_type=jnp.float32)
    router = jax.nn.softmax(logits, axis=-1)
    expert_hot = (expert_ids[:, :, None] == jnp.arange(EXPERTS)[None, None, :]).astype(jnp.float32)
    gate = jnp.sum(router[:, None, :] * expert_hot, axis=2)
    masks = route_masks(expert_ids, capacity)
    dispatch_float = jnp.sum(masks, axis=1)
    dispatch = dispatch_float.astype(jnp.bfloat16)
    combine = jnp.sum(masks * gate[:, :, None, None], axis=1)
    expert_rows = jnp.einsum(
        "rec,rd->ecd", dispatch, hidden2, preferred_element_type=jnp.float32
    ).astype(jnp.bfloat16)
    w_in_cols = lax.all_to_all(w_expert_in, "shard", 2, 1, tiled=True)
    grad = cotangent.astype(jnp.float32)
    grad_eout = jnp.einsum("rec,rd->ecd", combine, grad, precision=high).astype(jnp.bfloat16)
    gathered = lax.all_gather(jnp.stack([expert_rows, grad_eout]), "shard", axis=2, tiled=True)
    rows_all, geout_all = (gathered[0], gathered[1])
    pre = jnp.einsum("erd,edh->erh", rows_all, w_in_cols, preferred_element_type=jnp.float32)
    activated = jax.nn.gelu(pre, approximate=False).astype(jnp.bfloat16)
    out_part = jnp.einsum(
        "erh,ehd->erd", activated, w_expert_out, preferred_element_type=jnp.float32
    ).astype(jnp.bfloat16)
    grad_act = jnp.einsum(
        "erd,ehd->erh", geout_all, w_expert_out, preferred_element_type=jnp.float32
    )
    slope = (
        0.5 * (1.0 + jax.scipy.special.erf(pre * 0.7071067811865476))
        + pre * jnp.exp(-0.5 * pre * pre) * 0.3989422804014327
    )
    grad_pre = (grad_act * slope).astype(jnp.bfloat16)
    rows_part = jnp.einsum(
        "erh,edh->erd", grad_pre, w_in_cols, preferred_element_type=jnp.float32
    ).astype(jnp.bfloat16)
    scattered = lax.psum_scatter(
        jnp.stack([out_part, rows_part]), "shard", scatter_dimension=2, tiled=True
    )
    expert_out, grad_rows = (scattered[0], scattered[1])
    eout_float = expert_out.astype(jnp.float32)
    moe = jnp.einsum("rec,ecd->rd", combine, eout_float, precision=high)
    outputs = (attended + moe).astype(jnp.bfloat16)
    matched = jnp.einsum("rd,ecd->rec", grad, eout_float, precision=high)
    grad_gate = jnp.sum(masks * matched[:, None, :, :], axis=(2, 3))
    back_qkv, back_proj, back_router = (full_qkv, full_proj, full_router)
    gin_cols = jnp.einsum("erd,erh->edh", rows_all, grad_pre, preferred_element_type=jnp.float32)
    gin_local = lax.all_to_all(gin_cols.astype(jnp.bfloat16), "shard", 1, 2, tiled=True)
    gout_local = jnp.einsum(
        "erh,erd->ehd", activated, geout_all, preferred_element_type=jnp.float32
    ).astype(jnp.bfloat16)
    grad_probs = jnp.sum(grad_gate[:, :, None] * expert_hot, axis=1)
    grad_logits = (
        router * (grad_probs - jnp.sum(router * grad_probs, axis=-1, keepdims=True))
    ).astype(jnp.bfloat16)
    grad_hidden2 = jnp.einsum(
        "rec,ecd->rd", dispatch, grad_rows, preferred_element_type=jnp.float32
    ) + jnp.einsum("re,de->rd", grad_logits, back_router, preferred_element_type=jnp.float32)
    grad_norm2, gain2 = layer_norm_back(grad_hidden2, normed2, inverse2, norm2_gain)
    grad_attended = grad + grad_norm2
    grad_branch = grad_attended.astype(jnp.bfloat16)
    grad_mixed = jnp.einsum(
        "rk,dk->rd", grad_branch, back_proj, preferred_element_type=jnp.float32
    ).astype(jnp.bfloat16)
    grad_qkv_rows = attention_backward(qkv, mixed, logsum, grad_mixed, images)
    grad_hidden1 = jnp.einsum(
        "rk,dk->rd", grad_qkv_rows, back_qkv, preferred_element_type=jnp.float32
    )
    grad_norm1, gain1 = layer_norm_back(grad_hidden1, normed1, inverse1, norm1_gain)
    grad_inputs = grad_attended + grad_norm1
    n_shard = lax.axis_size("shard")
    n_rep = lax.axis_size("rep")
    gains = butterfly_sum(jnp.stack([gain1, gain2]), "shard", n_shard)
    gains = butterfly_sum(gains, "rep", n_rep)
    gain1_total, gain2_total = (gains[0], gains[1])
    dense_local = lax.psum_scatter(
        jnp.concatenate(
            [
                jnp.einsum("rc,rk->ck", hidden1, grad_qkv_rows, preferred_element_type=jnp.float32),
                jnp.einsum("rc,rk->ck", mixed, grad_branch, preferred_element_type=jnp.float32),
                jnp.einsum("rc,rk->ck", hidden2, grad_logits, preferred_element_type=jnp.float32),
            ],
            axis=1,
        ).astype(jnp.bfloat16),
        "shard",
        scatter_dimension=0,
        tiled=True,
    )
    dense_total, in_total, out_total = (
        butterfly_sum(dense_local, "rep", n_rep, jnp.bfloat16),
        butterfly_sum(gin_local, "rep", n_rep, jnp.bfloat16),
        butterfly_sum(gout_local, "rep", n_rep, jnp.bfloat16),
    )
    return (
        outputs,
        grad_inputs,
        gain1_total,
        dense_total[:, : 3 * width],
        dense_total[:, 3 * width : 4 * width],
        gain2_total,
        dense_total[:, 4 * width :],
        in_total,
        out_total,
    )


def solution(mesh):
    in_specs = (
        P(("shard", "rep"), None),
        P(),
        P("shard", None),
        P("shard", None),
        P(),
        P("shard", None),
        P(None, "shard", None),
        P(None, "shard", None),
        P(("shard", "rep"), None),
        P(),
        P(("shard", "rep"), None),
    )
    out_specs = (
        P(("shard", "rep"), None),
        P(("shard", "rep"), None),
        P(),
        P("shard", None),
        P("shard", None),
        P(),
        P("shard", None),
        P(None, "shard", None),
        P(None, "shard", None),
    )
    return jax.shard_map(body, mesh=mesh, in_specs=in_specs, out_specs=out_specs, check_vma=False)
```

profile of v0, /device:TPU:4, one launch (start us, length us, event | category | flops | bytes accessed | tf_op | source)
XLA Modules:
  0.0 680.0 jit_solution(1901787044144280053)
XLA Ops:
  17.6 79.0 %all-gather.3.cloned.1.call-done = bf16[768,3104]{1,0:T(8,128)(2,1)} async-done(((bf16[48,3104]{1,0:T(8,128)(2,1)}), bf16[768,3104]{1,0:T(8,128)(2,1)}) %all-gather.3.cloned.1.call-update) | async-done | bytes 4767760 | tf_op jit(solution)/shard_map/all_gather | solution.py:133
  96.6 3.1 convolution_convert_fusion.1
  115.4 4.3 copy.162
  119.7 4.1 reshape.249
  123.9 39.2 %all_to_all.36 = bf16[16,2,9216]{2,1,0:T(2,128)(2,1)} all-to-all(bf16[16,2,9216]{2,1,0:T(2,128)(2,1)} %reshape.249), channel_id=1, replica_groups=mesh['shard'=16,'rep'=16] {'shard'}, dimensions={0} | all-to-all | bytes 1179648 | tf_op jit(solution)/shard_map/all_to_all | solution.py:158
  163.1 3.3 reshape.250
  166.4 4.7 copy.163
  171.1 93.5 %all-gather.5.cloned.1.call-done = bf16[2,2,2048,768]{3,2,1,0:T(8,128)(2,1)} async-done(((bf16[2,2,128,768]{3,2,1,0:T(8,128)(2,1)}), bf16[2,2,2048,768]{3,2,1,0:T(8,128)(2,1)}) %all-gather.5.cloned.1.call-update) | async-done | bytes 12582928 | tf_op jit(solution)/shard_map/all_gather | solution.py:161
  264.6 5.5 fusion.34
  270.2 4.6 fusion.12
  277.0 7.2 %fusion.6 = bf16[2,2048,192]{1,2,0:T(8,128)(2,1)S(1)} fusion(f32[2,2048,192]{1,2,0:T(8,128)S(1)} %get-tuple-element.84, u8[2048,192]{0,1:T(8,128)(4,1)S(1)} %get-tuple-element.64, u8[2048,192]{0,1:T(8,128)(4,1)S(1)} %get-tuple-element.63), kind=kLoop, calls=%fused_computation.16 | loop fusion | flops 55050240 | bytes 5505024 | tf_op jit(solution)/shard_map/convert_element_type | solution.py:164
  286.1 5.6 pad_maximum_fusion
  292.0 170.9 %reduce-scatter.3.cloned.1.call-done = bf16[2,2,128,768]{3,2,1,0:T(8,128)(2,1)} async-done(((bf16[2,2,2048,768]{3,2,1,0:T(8,128)(2,1)}), bf16[2,2,128,768]{3,2,1,0:T(8,128)(2,1)}) %reduce-scatter.3.cloned.1.call-update) | async-done | bytes 786448 | tf_op jit(solution)/shard_map/reduce_scatter | solution.py:179
  464.3 2.7 fusion.49
  473.4 2.5 convolution_convert_fusion.7
  488.1 4.3 fusion.23
  493.9 4.5 fusion.24
  500.2 3.6 all-to-all-start.1
  503.9 3.5 collective-permute-done.16
  508.5 20.7 %all-to-all-done.1 = bf16[2,768,192]{2,0,1:T(2,128)(2,1)S(1)} async-done(((bf16[2,768,192]{2,0,1:T(2,128)(2,1)}), bf16[2,768,192]{2,0,1:T(2,128)(2,1)S(1)}, u32[]{:S(2)}, u32[]{:S(2)}) %all-to-all-start.1) | async-done | bytes 589856 | tf_op jit(solution)/shard_map/all_to_all | solution.py:190
  532.1 44.4 %collective-permute-done.17 = bf16[2,192,768]{2,1,0:T(8,128)(2,1)S(1)} collective-permute-done((bf16[2,192,768]{2,1,0:T(8,128)(2,1)S(1)}, bf16[2,192,768]{2,1,0:T(8,128)(2,1)S(1)}, u32[]{:S(2)}, u32[]{:S(2)}) %collective-permute-start.17) | collective-permute-done | bytes 589856 | tf_op jit(solution)/shard_map/ppermute | solution.py:37
  578.2 13.9 %collective-permute-done.18 = bf16[2,192,768]{2,1,0:T(8,128)(2,1)S(1)} collective-permute-done((bf16[2,192,768]{2,1,0:T(8,128)(2,1)S(1)}, bf16[2,192,768]{2,1,0:T(8,128)(2,1)S(1)}, u32[]{:S(2)}, u32[]{:S(2)}) %collective-permute-start.18) | collective-permute-done | bytes 589856 | tf_op jit(solution)/shard_map/ppermute | solution.py:37
  592.9 3.5 fusion.46
  596.6 15.5 %collective-permute-done.13 = bf16[2,48,3072]{2,1,0:T(8,128)(2,1)S(1)} collective-permute-done((bf16[2,48,3072]{2,1,0:T(8,128)(2,1)S(1)}, bf16[2,48,3072]{2,1,0:T(8,128)(2,1)S(1)}, u32[]{:S(2)}, u32[]{:S(2)}) %collective-permute-start.13) | collective-permute-done | bytes 589856 | tf_op jit(solution)/shard_map/ppermute | solution.py:37
  613.2 4.1 collective-permute-start.1
  622.2 5.5 collective-permute-done.14
  629.9 2.9 collective-permute-start.3
  634.0 10.9 %collective-permute-done.15 = bf16[2,48,3072]{2,1,0:T(8,128)(2,1)S(1)} collective-permute-done((bf16[2,48,3072]{2,1,0:T(8,128)(2,1)S(1)}, bf16[2,48,3072]{2,1,0:T(8,128)(2,1)S(1)}, u32[]{:S(2)}, u32[]{:S(2)}) %collective-permute-start.15) | collective-permute-done | bytes 589856 | tf_op jit(solution)/shard_map/ppermute | solution.py:37
  646.2 3.6 collective-permute-done.4
  651.8 2.5 collective-permute-done.5
  658.7 2.7 collective-permute-start.7
  664.5 6.5 collective-permute-done.11
  (211 shorter events, 82.3 us)
Async XLA Ops:
  7.2 263.0 %copy-start = (bf16[2,192,768]{2,1,0:T(8,128)(2,1)S(1)}, bf16[2,192,768]{2,1,0:T(8,128)(2,1)}, u32[]{:S(2)}) copy-start(bf16[2,192,768]{2,1,0:T(8,128)(2,1)} %param.18) | copy-start | bytes 1769476
  7.2 89.5 %all-gather.3.cloned.1.call-start = ((), (), s32[]{:S(2)}) async-start(), calls=%async_computation.4 | async-start | bytes 5222400 | tf_op jit(solution)/shard_map/all_gather | solution.py:133
  9.8 254.8 %all-gather.5.cloned.1.call-start = ((), (), s32[]{:S(2)}) async-start(), calls=%async_computation.5 | async-start | bytes 13369344 | tf_op jit(solution)/shard_map/all_gather | solution.py:161
  115.4 347.5 %reduce-scatter.3.cloned.1.call-start = ((), (), s32[]{:S(2)}) async-start(), calls=%async_computation.6 | async-start | bytes 13369344 | tf_op jit(solution)/shard_map/reduce_scatter | solution.py:179
  291.7 171.2 %copy-start.17 = (bf16[197,768]{1,0:T(8,128)(2,1)S(1)}, bf16[197,768]{1,0:T(8,128)(2,1)}, u32[]{:S(2)}) copy-start(bf16[197,768]{1,0:T(8,128)(2,1)} %param.21) | copy-start | bytes 907780
  291.7 172.6 %copy-start.22 = (f32[197,2,2]{2,1,0:T(2,128)S(1)}, f32[197,2,2]{2,1,0:T(2,128)}, u32[]{:S(2)}) copy-start(f32[197,2,2]{2,1,0:T(2,128)} %copy.157) | copy-start | bytes 9460
  291.8 330.5 %reduce-scatter.5.cloned.1.call-start = ((), (), s32[]{:S(2)}) async-start(), calls=%async_computation.7 | async-start | bytes 5222400 | tf_op jit(solution)/shard_map/reduce_scatter | solution.py:218
  492.4 15.0 %collective-permute-start.16 = (bf16[2,192,768]{2,1,0:T(8,128)(2,1)S(1)}, bf16[2,192,768]{2,1,0:T(8,128)(2,1)S(1)}, u32[]{:S(2)}, u32[]{:S(2)}) collective-permute-start(bf16[2,192,768]{2,1,0:T(8,128)(2,1)S(1)} %fusion.23), channel_id=1, source_target_pairs={{0,1},{1,0},{2,3},{3,2},{4,5},{5,4},{6,7},{7,6},{8,9},{9,8},{10,11... | collective-permute-start | bytes 1769480 | tf_op jit(solution)/shard_map/ppermute | solution.py:37
  500.2 29.0 %all-to-all-start.1 = ((bf16[2,768,192]{2,0,1:T(2,128)(2,1)}), bf16[2,768,192]{2,0,1:T(2,128)(2,1)S(1)}, u32[]{:S(2)}, u32[]{:S(2)}) async-start(bf16[2,768,192]{2,0,1:T(2,128)(2,1)} %copy.178), calls=%async_computation.3 | async-start | bytes 1572864 | tf_op jit(solution)/shard_map/all_to_all | solution.py:190
  507.5 69.0 %collective-permute-start.17 = (bf16[2,192,768]{2,1,0:T(8,128)(2,1)S(1)}, bf16[2,192,768]{2,1,0:T(8,128)(2,1)S(1)}, u32[]{:S(2)}, u32[]{:S(2)}) collective-permute-start(bf16[2,192,768]{2,1,0:T(8,128)(2,1)S(1)} %add_convert_fusion.2), channel_id=1, source_target_pairs={{0,2},{1,3},{2,0},{3,1},{4,6},{5,7},{6,4},{7,5},{8,10},{9,11},{10,... | collective-permute-start | bytes 1769480 | tf_op jit(solution)/shard_map/ppermute | solution.py:37
  530.4 62.5 %copy-start.28 = (bf16[12,64,197]{2,1,0:T(8,128)(2,1)S(1)}, bf16[12,64,197]{2,1,0:T(8,128)(2,1)}, u32[]{:S(2)}) copy-start(bf16[12,64,197]{2,1,0:T(8,128)(2,1)} %copy-done.27) | copy-start | bytes 907780
  530.4 62.5 %copy-start.30 = (bf16[12,64,197]{2,1,0:T(8,128)(2,1)S(1)}, bf16[12,64,197]{2,1,0:T(8,128)(2,1)}, u32[]{:S(2)}) copy-start(bf16[12,64,197]{2,1,0:T(8,128)(2,1)} %copy-done.29) | copy-start | bytes 907780
  530.4 47.6 %collective-permute-start.12 = (bf16[2,48,3072]{2,1,0:T(8,128)(2,1)S(1)}, bf16[2,48,3072]{2,1,0:T(8,128)(2,1)S(1)}, u32[]{:S(2)}, u32[]{:S(2)}) collective-permute-start(bf16[2,48,3072]{2,1,0:T(8,128)(2,1)S(1)} %all_to_all.33), channel_id=1, source_target_pairs={{0,1},{1,0},{2,3},{3,2},{4,5},{5,4},{6,7},{7,6},{8,9},{9,8},{10,11... | collective-permute-start | bytes 1769480 | tf_op jit(solution)/shard_map/ppermute | solution.py:37
  576.7 15.4 %collective-permute-start.18 = (bf16[2,192,768]{2,1,0:T(8,128)(2,1)S(1)}, bf16[2,192,768]{2,1,0:T(8,128)(2,1)S(1)}, u32[]{:S(2)}, u32[]{:S(2)}) collective-permute-start(bf16[2,192,768]{2,1,0:T(8,128)(2,1)S(1)} %add_convert_fusion.1), channel_id=1, source_target_pairs={{0,4},{1,5},{2,6},{3,7},{4,0},{5,1},{6,2},{7,3},{8,12},{9,13},{10,... | collective-permute-start | bytes 1769480 | tf_op jit(solution)/shard_map/ppermute | solution.py:37
  578.1 34.0 %collective-permute-start.13 = (bf16[2,48,3072]{2,1,0:T(8,128)(2,1)S(1)}, bf16[2,48,3072]{2,1,0:T(8,128)(2,1)S(1)}, u32[]{:S(2)}, u32[]{:S(2)}) collective-permute-start(bf16[2,48,3072]{2,1,0:T(8,128)(2,1)S(1)} %add_convert_fusion.5), channel_id=1, source_target_pairs={{0,2},{1,3},{2,0},{3,1},{4,6},{5,7},{6,4},{7,5},{8,10},{9,11},{10,... | collective-permute-start | bytes 1769480 | tf_op jit(solution)/shard_map/ppermute | solution.py:37
  592.3 25.0 %collective-permute-start.19 = (bf16[2,192,768]{2,1,0:T(8,128)(2,1)S(1)}, bf16[2,192,768]{2,1,0:T(8,128)(2,1)S(1)}, u32[]{:S(2)}, u32[]{:S(2)}) collective-permute-start(bf16[2,192,768]{2,1,0:T(8,128)(2,1)S(1)} %add_convert_fusion), channel_id=1, source_target_pairs={{0,8},{1,9},{2,10},{3,11},{4,12},{5,13},{6,14},{7,15},{8,0},{9,1},... | collective-permute-start | bytes 1769480 | tf_op jit(solution)/shard_map/ppermute | solution.py:37
  596.5 16.7 %collective-permute-start = (f32[2,768]{1,0:T(2,128)S(1)}, f32[2,768]{1,0:T(2,128)S(1)}, u32[]{:S(2)}, u32[]{:S(2)}) collective-permute-start(f32[2,768]{1,0:T(2,128)S(1)} %pad_maximum_fusion.7), channel_id=1, source_target_pairs={{0,16},{16,0},{32,48},{48,32},{64,80},{80,64},{96,112},{112,96},{1... | collective-permute-start | bytes 18440 | tf_op jit(solution)/shard_map/ppermute | solution.py:37
  612.3 15.4 %collective-permute-start.14 = (bf16[2,48,3072]{2,1,0:T(8,128)(2,1)S(1)}, bf16[2,48,3072]{2,1,0:T(8,128)(2,1)}, u32[]{:S(2)}, u32[]{:S(2)}) collective-permute-start(bf16[2,48,3072]{2,1,0:T(8,128)(2,1)S(1)} %add_convert_fusion.4), channel_id=1, source_target_pairs={{0,4},{1,5},{2,6},{3,7},{4,0},{5,1},{6,2},{7,3},{8,12},{9,13},{10,... | collective-permute-start | bytes 1769480 | tf_op jit(solution)/shard_map/ppermute | solution.py:37
  613.2 7.6 %collective-permute-start.1 = (f32[2,768]{1,0:T(2,128)S(1)}, f32[2,768]{1,0:T(2,128)S(1)}, u32[]{:S(2)}, u32[]{:S(2)}) collective-permute-start(f32[2,768]{1,0:T(2,128)S(1)} %fusion.72), channel_id=1, source_target_pairs={{0,32},{16,48},{32,0},{48,16},{64,96},{80,112},{96,64},{112,80},{1... | collective-permute-start | bytes 18440 | tf_op jit(solution)/shard_map/ppermute | solution.py:37
  618.4 36.8 %copy-start.6 = (f32[197,768]{1,0:T(8,128)S(1)}, f32[197,768]{1,0:T(8,128)}, u32[]{:S(2)}) copy-start(f32[197,768]{1,0:T(8,128)} %copy-done.4) | copy-start | bytes 1815556
  620.8 9.0 %collective-permute-start.2 = (f32[2,768]{1,0:T(2,128)S(1)}, f32[2,768]{1,0:T(2,128)S(1)}, u32[]{:S(2)}, u32[]{:S(2)}) collective-permute-start(f32[2,768]{1,0:T(2,128)S(1)} %fusion.102), channel_id=1, source_target_pairs={{0,64},{16,80},{32,96},{48,112},{64,0},{80,16},{96,32},{112,48},{1... | collective-permute-start | bytes 18440 | tf_op jit(solution)/shard_map/ppermute | solution.py:37
  622.2 10.6 %collective-permute-start.8 = (bf16[48,3104]{1,0:T(8,128)(2,1)}, bf16[48,3104]{1,0:T(8,128)(2,1)S(1)}, u32[]{:S(2)}, u32[]{:S(2)}) collective-permute-start(bf16[48,3104]{1,0:T(8,128)(2,1)} %reduce-scatter.5.cloned.1.call-done), channel_id=1, source_target_pairs={{0,1},{1,0},{2,3},{3,2},{4,5},{5,4},{6,7},{7,6},{8,9},{9,8},{10,11... | collective-permute-start | bytes 893960 | tf_op jit(solution)/shard_map/ppermute | solution.py:37
  628.9 16.0 %collective-permute-start.15 = (bf16[2,48,3072]{2,1,0:T(8,128)(2,1)S(1)}, bf16[2,48,3072]{2,1,0:T(8,128)(2,1)S(1)}, u32[]{:S(2)}, u32[]{:S(2)}) collective-permute-start(bf16[2,48,3072]{2,1,0:T(8,128)(2,1)S(1)} %add_convert_fusion.3), channel_id=1, source_target_pairs={{0,8},{1,9},{2,10},{3,11},{4,12},{5,13},{6,14},{7,15},{8,0},{9,1},... | collective-permute-start | bytes 1769480 | tf_op jit(solution)/shard_map/ppermute | solution.py:37
  629.9 16.2 %collective-permute-start.3 = (f32[2,768]{1,0:T(2,128)S(1)}, f32[2,768]{1,0:T(2,128)S(1)}, u32[]{:S(2)}, u32[]{:S(2)}) collective-permute-start(f32[2,768]{1,0:T(2,128)S(1)} %add.121), channel_id=1, source_target_pairs={{0,128},{16,144},{32,160},{48,176},{64,192},{80,208},{96,224},{112... | collective-permute-start | bytes 18440 | tf_op jit(solution)/shard_map/ppermute | solution.py:37
  633.9 28.6 %copy-start.3 = (f32[197,768]{1,0:T(8,128)S(1)}, f32[197,768]{1,0:T(8,128)}, u32[]{:S(2)}) copy-start(f32[197,768]{1,0:T(8,128)} %copy-done.2) | copy-start | bytes 1815556
  633.9 17.0 %collective-permute-start.9 = (bf16[48,3104]{1,0:T(8,128)(2,1)S(1)}, bf16[48,3104]{1,0:T(8,128)(2,1)S(1)}, u32[]{:S(2)}, u32[]{:S(2)}) collective-permute-start(bf16[48,3104]{1,0:T(8,128)(2,1)S(1)} %add_convert_fusion.8), channel_id=1, source_target_pairs={{0,2},{1,3},{2,0},{3,1},{4,6},{5,7},{6,4},{7,5},{8,10},{9,11},{10,... | collective-permute-start | bytes 893960 | tf_op jit(solution)/shard_map/ppermute | solution.py:37
  646.1 3.7 collective-permute-start.4
  649.8 4.5 collective-permute-start.5
  650.9 10.5 %collective-permute-start.10 = (bf16[48,3104]{1,0:T(8,128)(2,1)S(1)}, bf16[48,3104]{1,0:T(8,128)(2,1)S(1)}, u32[]{:S(2)}, u32[]{:S(2)}) collective-permute-start(bf16[48,3104]{1,0:T(8,128)(2,1)S(1)} %add_convert_fusion.7), channel_id=1, source_target_pairs={{0,4},{1,5},{2,6},{3,7},{4,0},{5,1},{6,2},{7,3},{8,12},{9,13},{10,... | collective-permute-start | bytes 893960 | tf_op jit(solution)/shard_map/ppermute | solution.py:37
  654.3 4.4 collective-permute-start.6
  658.7 5.1 collective-permute-start.7
  661.5 9.5 %collective-permute-start.11 = (bf16[48,3104]{1,0:T(8,128)(2,1)S(1)}, bf16[48,3104]{1,0:T(8,128)(2,1)S(1)}, u32[]{:S(2)}, u32[]{:S(2)}) collective-permute-start(bf16[48,3104]{1,0:T(8,128)(2,1)S(1)} %add_convert_fusion.6), channel_id=1, source_target_pairs={{0,8},{1,9},{2,10},{3,11},{4,12},{5,13},{6,14},{7,15},{8,0},{9,1},... | collective-permute-start | bytes 893960 | tf_op jit(solution)/shard_map/ppermute | solution.py:37
  (27 other events, 128.8 us)
Sparse Core Ops, SparseCore 0:
  11.2 85.3 all-gather.2
  115.5 149.0 all-gather.4
  291.9 170.9 reduce-scatter.2
  486.8 124.1 reduce-scatter.4
where the time goes:
time: 687 us; the launch traced here: 680 us
  waiting for transfers between devices  476 us (69%)
  matrix products  49.8 us (7%)
  blocking collectives  39.2 us (6%)
  other arithmetic  37.6 us (5%)
  local copies, waits for them, and re-layouts  35.7 us (5%)
  starting transfers between devices  27.2 us (4%)
  between operations  14.8 us (2%)
    reduce_scatter x1, waiting for transfers between devices, body(): lax.psum_scatter(jnp.stack([out_part, rows_part]), 'shard', scatter_dimen...  171 us
    ppermute x20, waiting for transfers between devices, butterfly_sum(): other = lax.ppermute(sent, axis, pairs)  111 us
    all_gather x1, waiting for transfers between devices, body(): lax.all_gather(jnp.stack([expert_rows, grad_eout]), 'shard', axis=2, tile...  93.5 us
    all_gather x1, waiting for transfers between devices, body(): lax.all_gather(jnp.concatenate([w_qkv, w_proj, w_router], axis=1), 'shard...  79 us
    all_to_all x1, blocking collectives, body(): w_in_cols = lax.all_to_all(w_expert_in, 'shard', 2, 1, tiled=True)  39.2 us
    ppermute x20, starting transfers between devices, butterfly_sum(): other = lax.ppermute(sent, axis, pairs)  23.2 us
    all_to_all x1, waiting for transfers between devices, body(): lax.all_to_all(gin_cols.astype(jnp.bfloat16), 'shard', 1, 2, tiled=True)  20.7 us
    unnamed x74, local copies, waits for them, and re-layouts  16.6 us
  transfers between devices with their start and end apart: 25, of which 16 were waited for; matrix products, arithmetic and copies ran while one was open for 7% of the time, Pallas kernels for 0%

commit v1 on v0

--- a/solution.py
+++ b/solution.py
@@ -158,7 +158,12 @@
     w_in_cols = lax.all_to_all(w_expert_in, "shard", 2, 1, tiled=True)
     grad = cotangent.astype(jnp.float32)
     grad_eout = jnp.einsum("rec,rd->ecd", combine, grad, precision=high).astype(jnp.bfloat16)
-    gathered = lax.all_gather(jnp.stack([expert_rows, grad_eout]), "shard", axis=2, tiled=True)
+    gathered = jnp.concatenate(
+        lax.all_to_all(
+            jnp.stack([jnp.stack([expert_rows, grad_eout])] * lax.axis_size("shard")), "shard", 0, 0
+        ),
+        axis=2,
+    )
     rows_all, geout_all = (gathered[0], gathered[1])
     pre = jnp.einsum("erd,edh->erh", rows_all, w_in_cols, preferred_element_type=jnp.float32)
     activated = jax.nn.gelu(pre, approximate=False).astype(jnp.bfloat16)

time: 687 us -> 859 us (1.25)
  waiting for transfers between devices: 476 us -> 654 us
  blocking collectives: 39.2 us -> 0 us
  starting transfers between devices: 27.2 us -> 47.4 us
  local copies, waits for them, and re-layouts: 35.7 us -> 51.6 us
    all_to_all x0 -> x2, waiting for transfers between devices: none -> 280 us  [the longest x1 280 us: body(): lax.all_to_all(jnp.stack([jnp.stack([expert_rows, grad_eout])] * lax.axis...]
    all_gather x1 -> x0, waiting for transfers between devices: 93.5 us -> none  [body(): lax.all_gather(jnp.stack([expert_rows, grad_eout]), 'shard', axis=2, tile...]
    all_to_all x1 -> x0, blocking collectives: 39.2 us -> none  [body(): w_in_cols = lax.all_to_all(w_expert_in, 'shard', 2, 1, tiled=True)]
    all_to_all x0 -> x2, starting transfers between devices: none -> 16.2 us  [the longest x1 11.2 us: body(): w_in_cols = lax.all_to_all(w_expert_in, 'shard', 2, 1, tiled=True)]
    slice x1 -> x4, local copies, waits for them, and re-layouts: 0.21 us -> 9.42 us  [the longest x3 9.21 us: body(): rows_all, geout_all = (gathered[0], gathered[1])]
  transfers between devices with their start and end apart: 25 -> 26, of which waited for: 16 -> 17; matrix products, arithmetic and copies ran while one was open for 7% -> 7% of each run, Pallas kernels for 0% -> 0%
where the time goes in v1:
time: 859 us; the launch traced here: 849 us
  waiting for transfers between devices  654 us (76%)
  local copies, waits for them, and re-layouts  51.6 us (6%)
  starting transfers between devices  47.4 us (6%)
  matrix products  46.3 us (5%)
  other arithmetic  35.6 us (4%)
  between operations  15 us (2%)
    all_to_all x1, waiting for transfers between devices, body(): lax.all_to_all(jnp.stack([jnp.stack([expert_rows, grad_eout])] * lax.axis...  280 us
    reduce_scatter x1, waiting for transfers between devices, body(): lax.psum_scatter(jnp.stack([out_part, rows_part]), 'shard', scatter_dimen...  176 us
    ppermute x20, waiting for transfers between devices, butterfly_sum(): other = lax.ppermute(sent, axis, pairs)  107 us
    all_gather x1, waiting for transfers between devices, body(): lax.all_gather(jnp.concatenate([w_qkv, w_proj, w_router], axis=1), 'shard...  74 us
    ppermute x20, starting transfers between devices, butterfly_sum(): other = lax.ppermute(sent, axis, pairs)  26.8 us
  transfers between devices with their start and end apart: 26, of which 17 were waited for; matrix products, arithmetic and copies ran while one was open for 7% of the time, Pallas kernels for 0%

profile of v1, /device:TPU:4, one launch (start us, length us, event | category | flops | bytes accessed | tf_op | source)
XLA Modules:
  0.0 849.4 jit_solution(2476435747398327314)
XLA Ops:
  9.8 3.7 copy.167
  13.5 3.1 reshape.260
  16.6 11.2 %all-to-all-start.1 = ((bf16[16,2,9216]{2,1,0:T(2,128)(2,1)}), bf16[16,2,9216]{2,1,0:T(2,128)(2,1)}, u32[]{:S(2)}, u32[]{:S(2)}) async-start(bf16[16,2,9216]{2,1,0:T(2,128)(2,1)} %reshape.260), calls=%async_computation.1 | async-start | bytes 1179648 | tf_op jit(solution)/shard_map/all_to_all | solution.py:158
  31.7 74.0 %all-gather.2.cloned.1.call-done = bf16[768,3104]{1,0:T(8,128)(2,1)} async-done(((bf16[48,3104]{1,0:T(8,128)(2,1)}), bf16[768,3104]{1,0:T(8,128)(2,1)}) %all-gather.2.cloned.1.call-update) | async-done | bytes 4767760 | tf_op jit(solution)/shard_map/all_gather | solution.py:133
  124.3 7.1 stack.23
  131.4 4.9 all-to-all-start
  136.8 3.3 reshape.261
  140.2 4.7 copy.168
  144.9 280.2 %all-to-all-done = bf16[16,2,2,128,768]{4,3,2,1,0:T(8,128)(2,1)} async-done(((bf16[16,2,2,128,768]{4,3,2,1,0:T(8,128)(2,1)}), bf16[16,2,2,128,768]{4,3,2,1,0:T(8,128)(2,1)}, u32[]{:S(2)}, u32[]{:S(2)}) %all-to-all-start) | async-done | bytes 12582944 | tf_op jit(solution)/shard_map/all_to_all | solution.py:162
  425.1 5.6 fusion.69
  430.7 3.0 copy.170
  434.8 4.5 fusion.28
  440.5 4.0 fusion.8
  447.0 7.2 fusion.2
  456.1 5.7 pad_maximum_fusion
  462.1 175.9 %reduce-scatter.3.cloned.1.call-done = bf16[2,2,128,768]{3,2,1,0:T(8,128)(2,1)} async-done(((bf16[2,2,2048,768]{3,2,1,0:T(8,128)(2,1)}), bf16[2,2,128,768]{3,2,1,0:T(8,128)(2,1)}) %reduce-scatter.3.cloned.1.call-update) | async-done | bytes 786448 | tf_op jit(solution)/shard_map/reduce_scatter | solution.py:184
  661.9 4.8 convolution_convert_fusion.4
  670.6 3.1 copy.184
  673.7 3.6 all-to-all-start.2
  677.3 8.1 collective-permute-done.16
  686.9 16.4 %all-to-all-done.2 = bf16[2,768,192]{2,0,1:T(2,128)(2,1)S(1)} async-done(((bf16[2,768,192]{2,0,1:T(2,128)(2,1)}), bf16[2,768,192]{2,0,1:T(2,128)(2,1)S(1)}, u32[]{:S(2)}, u32[]{:S(2)}) %all-to-all-start.2) | async-done | bytes 589856 | tf_op jit(solution)/shard_map/all_to_all | solution.py:195
  705.6 44.9 %collective-permute-done.17 = bf16[2,192,768]{2,1,0:T(8,128)(2,1)S(1)} collective-permute-done((bf16[2,192,768]{2,1,0:T(8,128)(2,1)S(1)}, bf16[2,192,768]{2,1,0:T(8,128)(2,1)S(1)}, u32[]{:S(2)}, u32[]{:S(2)}) %collective-permute-start.17) | collective-permute-done | bytes 589856 | tf_op jit(solution)/shard_map/ppermute | solution.py:37
  752.3 13.8 %collective-permute-done.18 = bf16[2,192,768]{2,1,0:T(8,128)(2,1)S(1)} collective-permute-done((bf16[2,192,768]{2,1,0:T(8,128)(2,1)S(1)}, bf16[2,192,768]{2,1,0:T(8,128)(2,1)S(1)}, u32[]{:S(2)}, u32[]{:S(2)}) %collective-permute-start.18) | collective-permute-done | bytes 589856 | tf_op jit(solution)/shard_map/ppermute | solution.py:37
  766.9 3.5 fusion.40
  770.6 13.4 %collective-permute-done.13 = bf16[2,48,3072]{2,1,0:T(8,128)(2,1)S(1)} collective-permute-done((bf16[2,48,3072]{2,1,0:T(8,128)(2,1)S(1)}, bf16[2,48,3072]{2,1,0:T(8,128)(2,1)S(1)}, u32[]{:S(2)}, u32[]{:S(2)}) %collective-permute-start.13) | collective-permute-done | bytes 589856 | tf_op jit(solution)/shard_map/ppermute | solution.py:37
  785.1 3.4 collective-permute-start.1
  789.6 3.1 collective-permute-done.1
  793.9 5.4 collective-permute-start.8
  809.6 7.2 collective-permute-done.15
  818.1 4.4 collective-permute-done.4
  823.5 3.5 collective-permute-done.5
  836.7 3.7 collective-permute-done.11
  (250 shorter events, 93.9 us)
Async XLA Ops:
  7.2 432.2 %copy-start = (bf16[2,192,768]{2,1,0:T(8,128)(2,1)S(1)}, bf16[2,192,768]{2,1,0:T(8,128)(2,1)}, u32[]{:S(2)}) copy-start(bf16[2,192,768]{2,1,0:T(8,128)(2,1)} %param.18) | copy-start | bytes 1769476
  7.2 98.4 %all-gather.2.cloned.1.call-start = ((), (), s32[]{:S(2)}) async-start(), calls=%async_computation.5 | async-start | bytes 5222400 | tf_op jit(solution)/shard_map/all_gather | solution.py:133
  16.6 107.6 %all-to-all-start.1 = ((bf16[16,2,9216]{2,1,0:T(2,128)(2,1)}), bf16[16,2,9216]{2,1,0:T(2,128)(2,1)}, u32[]{:S(2)}, u32[]{:S(2)}) async-start(bf16[16,2,9216]{2,1,0:T(2,128)(2,1)} %reshape.260), calls=%async_computation.1 | async-start | bytes 1179648 | tf_op jit(solution)/shard_map/all_to_all | solution.py:158
  131.4 293.7 %all-to-all-start = ((bf16[16,2,2,128,768]{4,3,2,1,0:T(8,128)(2,1)}), bf16[16,2,2,128,768]{4,3,2,1,0:T(8,128)(2,1)}, u32[]{:S(2)}, u32[]{:S(2)}) async-start(bf16[16,2,2,128,768]{4,3,2,1,0:T(8,128)(2,1)} %stack.23), calls=%async_computation | async-start | bytes 25165824 | tf_op jit(solution)/shard_map/all_to_all | solution.py:162
  136.3 501.7 %reduce-scatter.3.cloned.1.call-start = ((), (), s32[]{:S(2)}) async-start(), calls=%async_computation.6 | async-start | bytes 13369344 | tf_op jit(solution)/shard_map/reduce_scatter | solution.py:184
  461.8 176.2 %copy-start.19 = (bf16[197,768]{1,0:T(8,128)(2,1)S(1)}, bf16[197,768]{1,0:T(8,128)(2,1)}, u32[]{:S(2)}) copy-start(bf16[197,768]{1,0:T(8,128)(2,1)} %param.21) | copy-start | bytes 907780
  461.8 177.6 %copy-start.25 = (f32[197,2,2]{2,1,0:T(2,128)S(1)}, f32[197,2,2]{2,1,0:T(2,128)}, u32[]{:S(2)}) copy-start(f32[197,2,2]{2,1,0:T(2,128)} %copy.161) | copy-start | bytes 9460
  461.8 182.8 %copy-start.37 = (f32[768]{0:T(1024)S(1)}, f32[768]{0:T(1024)}, u32[]{:S(2)}) copy-start(f32[768]{0:T(1024)} %param.15) | copy-start | bytes 9220
  461.8 182.8 %copy-start.39 = (f32[197]{0:T(256)S(1)}, f32[197]{0:T(256)}, u32[]{:S(2)}) copy-start(f32[197]{0:T(256)} %copy-done.38) | copy-start | bytes 2368
  461.8 182.8 %copy-start.41 = (f32[197]{0:T(256)S(1)}, f32[197]{0:T(256)}, u32[]{:S(2)}) copy-start(f32[197]{0:T(256)} %copy-done.40) | copy-start | bytes 2368
  461.9 332.1 %reduce-scatter.5.cloned.1.call-start = ((), (), s32[]{:S(2)}) async-start(), calls=%async_computation.7 | async-start | bytes 5222400 | tf_op jit(solution)/shard_map/reduce_scatter | solution.py:223
  666.8 18.7 %collective-permute-start.16 = (bf16[2,192,768]{2,1,0:T(8,128)(2,1)S(1)}, bf16[2,192,768]{2,1,0:T(8,128)(2,1)}, u32[]{:S(2)}, u32[]{:S(2)}) collective-permute-start(bf16[2,192,768]{2,1,0:T(8,128)(2,1)S(1)} %convolution_convert_fusion.4), channel_id=1, source_target_pairs={{0,1},{1,0},{2,3},{3,2},{4,5},{5,4},{6,7},{7,6},{8,9},{9,8},{10,11... | collective-permute-start | bytes 1769480 | tf_op jit(solution)/shard_map/ppermute | solution.py:37
  673.7 29.6 %all-to-all-start.2 = ((bf16[2,768,192]{2,0,1:T(2,128)(2,1)}), bf16[2,768,192]{2,0,1:T(2,128)(2,1)S(1)}, u32[]{:S(2)}, u32[]{:S(2)}) async-start(bf16[2,768,192]{2,0,1:T(2,128)(2,1)} %copy.184), calls=%async_computation.4 | async-start | bytes 1572864 | tf_op jit(solution)/shard_map/all_to_all | solution.py:195
  686.8 63.7 %collective-permute-start.17 = (bf16[2,192,768]{2,1,0:T(8,128)(2,1)S(1)}, bf16[2,192,768]{2,1,0:T(8,128)(2,1)S(1)}, u32[]{:S(2)}, u32[]{:S(2)}) collective-permute-start(bf16[2,192,768]{2,1,0:T(8,128)(2,1)S(1)} %add_convert_fusion.2), channel_id=1, source_target_pairs={{0,2},{1,3},{2,0},{3,1},{4,6},{5,7},{6,4},{7,5},{8,10},{9,11},{10,... | collective-permute-start | bytes 1769480 | tf_op jit(solution)/shard_map/ppermute | solution.py:37
  704.5 47.5 %collective-permute-start.12 = (bf16[2,48,3072]{2,1,0:T(8,128)(2,1)S(1)}, bf16[2,48,3072]{2,1,0:T(8,128)(2,1)S(1)}, u32[]{:S(2)}, u32[]{:S(2)}) collective-permute-start(bf16[2,48,3072]{2,1,0:T(8,128)(2,1)S(1)} %all_to_all.37), channel_id=1, source_target_pairs={{0,1},{1,0},{2,3},{3,2},{4,5},{5,4},{6,7},{7,6},{8,9},{9,8},{10,11... | collective-permute-start | bytes 1769480 | tf_op jit(solution)/shard_map/ppermute | solution.py:37
  750.7 15.4 %collective-permute-start.18 = (bf16[2,192,768]{2,1,0:T(8,128)(2,1)S(1)}, bf16[2,192,768]{2,1,0:T(8,128)(2,1)S(1)}, u32[]{:S(2)}, u32[]{:S(2)}) collective-permute-start(bf16[2,192,768]{2,1,0:T(8,128)(2,1)S(1)} %add_convert_fusion.1), channel_id=1, source_target_pairs={{0,4},{1,5},{2,6},{3,7},{4,0},{5,1},{6,2},{7,3},{8,12},{9,13},{10,... | collective-permute-start | bytes 1769480 | tf_op jit(solution)/shard_map/ppermute | solution.py:37
  752.2 31.8 %collective-permute-start.13 = (bf16[2,48,3072]{2,1,0:T(8,128)(2,1)S(1)}, bf16[2,48,3072]{2,1,0:T(8,128)(2,1)S(1)}, u32[]{:S(2)}, u32[]{:S(2)}) collective-permute-start(bf16[2,48,3072]{2,1,0:T(8,128)(2,1)S(1)} %add_convert_fusion.5), channel_id=1, source_target_pairs={{0,2},{1,3},{2,0},{3,1},{4,6},{5,7},{6,4},{7,5},{8,10},{9,11},{10,... | collective-permute-start | bytes 1769480 | tf_op jit(solution)/shard_map/ppermute | solution.py:37
  766.2 22.3 %collective-permute-start.19 = (bf16[2,192,768]{2,1,0:T(8,128)(2,1)S(1)}, bf16[2,192,768]{2,1,0:T(8,128)(2,1)S(1)}, u32[]{:S(2)}, u32[]{:S(2)}) collective-permute-start(bf16[2,192,768]{2,1,0:T(8,128)(2,1)S(1)} %add_convert_fusion), channel_id=1, source_target_pairs={{0,8},{1,9},{2,10},{3,11},{4,12},{5,13},{6,14},{7,15},{8,0},{9,1},... | collective-permute-start | bytes 1769480 | tf_op jit(solution)/shard_map/ppermute | solution.py:37
  770.5 14.6 %collective-permute-start = (f32[2,768]{1,0:T(2,128)S(1)}, f32[2,768]{1,0:T(2,128)S(1)}, u32[]{:S(2)}, u32[]{:S(2)}) collective-permute-start(f32[2,768]{1,0:T(2,128)S(1)} %pad_maximum_fusion.7), channel_id=1, source_target_pairs={{0,16},{16,0},{32,48},{48,32},{64,80},{80,64},{96,112},{112,96},{1... | collective-permute-start | bytes 18440 | tf_op jit(solution)/shard_map/ppermute | solution.py:37
  784.1 15.4 %collective-permute-start.14 = (bf16[2,48,3072]{2,1,0:T(8,128)(2,1)S(1)}, bf16[2,48,3072]{2,1,0:T(8,128)(2,1)}, u32[]{:S(2)}, u32[]{:S(2)}) collective-permute-start(bf16[2,48,3072]{2,1,0:T(8,128)(2,1)S(1)} %add_convert_fusion.4), channel_id=1, source_target_pairs={{0,4},{1,5},{2,6},{3,7},{4,0},{5,1},{6,2},{7,3},{8,12},{9,13},{10,... | collective-permute-start | bytes 1769480 | tf_op jit(solution)/shard_map/ppermute | solution.py:37
  785.1 7.6 collective-permute-start.1
  792.7 8.9 %collective-permute-start.2 = (f32[2,768]{1,0:T(2,128)S(1)}, f32[2,768]{1,0:T(2,128)S(1)}, u32[]{:S(2)}, u32[]{:S(2)}) collective-permute-start(f32[2,768]{1,0:T(2,128)S(1)} %fusion.101), channel_id=1, source_target_pairs={{0,64},{16,80},{32,96},{48,112},{64,0},{80,16},{96,32},{112,48},{1... | collective-permute-start | bytes 18440 | tf_op jit(solution)/shard_map/ppermute | solution.py:37
  793.9 12.1 %collective-permute-start.8 = (bf16[48,3104]{1,0:T(8,128)(2,1)}, bf16[48,3104]{1,0:T(8,128)(2,1)S(1)}, u32[]{:S(2)}, u32[]{:S(2)}) collective-permute-start(bf16[48,3104]{1,0:T(8,128)(2,1)} %reduce-scatter.5.cloned.1.call-done), channel_id=1, source_target_pairs={{0,1},{1,0},{2,3},{3,2},{4,5},{5,4},{6,7},{7,6},{8,9},{9,8},{10,11... | collective-permute-start | bytes 893960 | tf_op jit(solution)/shard_map/ppermute | solution.py:37
  800.8 16.0 %collective-permute-start.15 = (bf16[2,48,3072]{2,1,0:T(8,128)(2,1)S(1)}, bf16[2,48,3072]{2,1,0:T(8,128)(2,1)S(1)}, u32[]{:S(2)}, u32[]{:S(2)}) collective-permute-start(bf16[2,48,3072]{2,1,0:T(8,128)(2,1)S(1)} %add_convert_fusion.3), channel_id=1, source_target_pairs={{0,8},{1,9},{2,10},{3,11},{4,12},{5,13},{6,14},{7,15},{8,0},{9,1},... | collective-permute-start | bytes 1769480 | tf_op jit(solution)/shard_map/ppermute | solution.py:37
  801.6 16.3 %collective-permute-start.3 = (f32[2,768]{1,0:T(2,128)S(1)}, f32[2,768]{1,0:T(2,128)S(1)}, u32[]{:S(2)}, u32[]{:S(2)}) collective-permute-start(f32[2,768]{1,0:T(2,128)S(1)} %add.121), channel_id=1, source_target_pairs={{0,128},{16,144},{32,160},{48,176},{64,192},{80,208},{96,224},{112... | collective-permute-start | bytes 18440 | tf_op jit(solution)/shard_map/ppermute | solution.py:37
  807.1 15.3 %collective-permute-start.9 = (bf16[48,3104]{1,0:T(8,128)(2,1)S(1)}, bf16[48,3104]{1,0:T(8,128)(2,1)S(1)}, u32[]{:S(2)}, u32[]{:S(2)}) collective-permute-start(bf16[48,3104]{1,0:T(8,128)(2,1)S(1)} %add_convert_fusion.8), channel_id=1, source_target_pairs={{0,2},{1,3},{2,0},{3,1},{4,6},{5,7},{6,4},{7,5},{8,10},{9,11},{10,... | collective-permute-start | bytes 893960 | tf_op jit(solution)/shard_map/ppermute | solution.py:37
  818.0 4.5 collective-permute-start.4
  822.4 4.5 collective-permute-start.5
  822.5 9.3 %collective-permute-start.10 = (bf16[48,3104]{1,0:T(8,128)(2,1)S(1)}, bf16[48,3104]{1,0:T(8,128)(2,1)S(1)}, u32[]{:S(2)}, u32[]{:S(2)}) collective-permute-start(bf16[48,3104]{1,0:T(8,128)(2,1)S(1)} %add_convert_fusion.7), channel_id=1, source_target_pairs={{0,4},{1,5},{2,6},{3,7},{4,0},{5,1},{6,2},{7,3},{8,12},{9,13},{10,... | collective-permute-start | bytes 893960 | tf_op jit(solution)/shard_map/ppermute | solution.py:37
  827.0 3.9 collective-permute-start.6
  830.9 5.3 collective-permute-start.7
  831.9 8.6 %collective-permute-start.11 = (bf16[48,3104]{1,0:T(8,128)(2,1)S(1)}, bf16[48,3104]{1,0:T(8,128)(2,1)S(1)}, u32[]{:S(2)}, u32[]{:S(2)}) collective-permute-start(bf16[48,3104]{1,0:T(8,128)(2,1)S(1)} %add_convert_fusion.6), channel_id=1, source_target_pairs={{0,8},{1,9},{2,10},{3,11},{4,12},{5,13},{6,14},{7,15},{8,0},{9,1},... | collective-permute-start | bytes 893960 | tf_op jit(solution)/shard_map/ppermute | solution.py:37
  (45 other events, 653.8 us)
Sparse Core Ops, SparseCore 0:
  11.2 94.3 all-gather.1
  461.9 176.0 reduce-scatter.2
  662.0 127.3 reduce-scatter.4
